TPU v7x, 32 devices: a whole 2x2x4 slice. The times are simulated.
32 devices in a mesh: row: 4 (over x, core), col: 8 (over z, y).
Axes of the slice: x: 2, y: 2, z: 4, core: 2. Of those that a mesh axis runs over, the one named last changes fastest.
Arguments:
- features: bfloat16 [4096, 256], P(('row', 'col')), may hold values from -192 to 192
- grad_out: bfloat16 [4096, 256], P(('row', 'col')), may hold values from -192 to 192
- tile_weight: bfloat16 [2048, 128, 128], P(('row', 'col')), may hold values from 0 to 256, as said below
- tile_list: int32 [128, 3, 32], P(('row', 'col')), may hold values from -1 to 63, as said below
Outputs:
- aggregated: bfloat16 [4096, 256], P(('row', 'col'))
- feature_grad: bfloat16 [4096, 256], P(('row', 'col'))
Inputs may be any that keep to these rules, and one draw needn't show every extreme that they name: `tile_list`: each column of a list is a slot (tile number, source block below 1, destination block below 8); tile number -1 marks an empty slot, whose blocks are 0. The tile numbers listed by one device are distinct and are 0 to n - 1 for some n between 40 and 64; some device lists all 64. On every device some step has all 32 slots used. Stored tiles that no slot lists take no part. `tile_weight`: entries are whole numbers.
All inputs are finite; a program needn't handle non-finite values.
Results may differ from a plain program's by a relative error of at most 0.017.
Values may be sent and summed in bfloat16 or wider, within the bound.
No kernel may reach another device: no remote copies, remote signals or barrier semaphores. Data moves between devices by JAX's collectives and lax.ppermute only.
A program may use at most 64 MiB of HBM per device.

v0:
```python
import math
import jax
import jax.numpy as jnp
from jax import lax
from jax.sharding import PartitionSpec as P


def passed_along(value, axis, steps):
    count = lax.axis_size(axis)
    pairs = [(source, (source + steps) % count) for source in range(count)]
    return lax.ppermute(value, axis, pairs)


def local(features, grad_out, tile_weight, tile_list):
    step_count = lax.axis_size("row")
    columns = lax.axis_size("col")
    row_pos = lax.axis_index("row")
    slot_count = tile_list.shape[2]
    tiles_here = tile_weight.shape[0]
    tile_len = tile_weight.shape[1]
    feat_width = features.shape[1]
    src_blocks = features.shape[0] // tile_len
    dst_blocks = columns * (grad_out.shape[0] // tile_len)
    flat_ids = tile_list[:, 0, :].reshape(-1)
    flat_step = jnp.arange(step_count * slot_count, dtype=jnp.int32) // slot_count
    matches = (flat_ids[None, :] == jnp.arange(tiles_here, dtype=jnp.int32)[:, None]).astype(
        jnp.int32
    )
    tile_used = jnp.sum(matches, axis=1)
    tile_step = jnp.sum(matches * flat_step[None, :], axis=1)
    tile_src = jnp.sum(matches * tile_list[:, 1, :].reshape(-1)[None, :], axis=1)
    tile_dst = jnp.sum(matches * tile_list[:, 2, :].reshape(-1)[None, :], axis=1)
    owner_row = (row_pos - tile_step) % step_count
    src_slot = owner_row * src_blocks + tile_src
    used_float = tile_used.astype(jnp.float32)
    row_sums = jnp.sum(tile_weight, axis=2, dtype=jnp.float32)
    col_sums = jnp.sum(tile_weight, axis=1, dtype=jnp.float32)
    dst_pick = (tile_dst[:, None] == jnp.arange(dst_blocks, dtype=jnp.int32)[None, :]).astype(
        jnp.float32
    ) * used_float[:, None]
    src_pick = (
        src_slot[:, None] == jnp.arange(step_count * src_blocks, dtype=jnp.int32)[None, :]
    ).astype(jnp.float32) * used_float[:, None]
    dst_terms = jnp.dot(dst_pick.T, row_sums, precision=lax.Precision.HIGHEST).reshape(-1)
    src_terms = jnp.dot(src_pick.T, col_sums, precision=lax.Precision.HIGHEST).reshape(-1)
    src_scale = lax.rsqrt(1.0 + lax.psum_scatter(src_terms, "row", scatter_dimension=0, tiled=True))
    dst_scale = lax.rsqrt(1.0 + lax.psum_scatter(dst_terms, "col", scatter_dimension=0, tiled=True))
    scaled = (features.astype(jnp.float32) * src_scale[:, None]).astype(jnp.bfloat16)
    scaled = scaled.reshape(src_blocks, tile_len, feat_width)
    scaled_grads = (grad_out.astype(jnp.float32) * dst_scale[:, None]).astype(jnp.bfloat16)
    grad_rows = lax.all_gather(scaled_grads, "col", axis=0, tiled=True).reshape(
        dst_blocks, tile_len, feat_width
    )

    def pick_tiles(list_step):
        tile_ids = tile_list[list_step, 0]
        keep_mask = (tile_ids >= 0).astype(jnp.bfloat16)
        chosen = tile_weight[jnp.maximum(tile_ids, 0)] * keep_mask[:, None, None]
        return (chosen, tile_list[list_step, 1], tile_list[list_step, 2])

    def backward_add(accum_total, rows, list_step):
        chosen, src_index, dst_index = pick_tiles(list_step)
        products = jnp.einsum(
            "kij,kif->kjf", chosen, rows[dst_index], preferred_element_type=jnp.float32
        )
        return accum_total.at[src_index].add(products)

    def grad_step(grad_state, step_pos):
        return backward_add(grad_state, grad_rows, step_count - 1 - step_pos)

    def grad_move(grad_state):
        return passed_along(grad_state.astype(jnp.bfloat16), "row", -1).astype(grad_state.dtype)

    partial_zero = jnp.zeros((dst_blocks, tile_len, feat_width), jnp.float32)
    everything = lax.all_gather(scaled, "row", axis=0, tiled=True)
    batch_size = math.gcd(tiles_here, 16)

    def tile_batch(loop_index, partial_value):
        first_tile = loop_index * batch_size
        tile_block = lax.dynamic_slice_in_dim(tile_weight, first_tile, batch_size, 0)
        keep_mask = lax.dynamic_slice_in_dim(tile_used, first_tile, batch_size, 0).astype(
            jnp.bfloat16
        )
        src_index = lax.dynamic_slice_in_dim(src_slot, first_tile, batch_size, 0)
        dst_index = lax.dynamic_slice_in_dim(tile_dst, first_tile, batch_size, 0)
        chosen = tile_block * keep_mask[:, None, None]
        products = jnp.einsum(
            "kij,kjf->kif", chosen, everything[src_index], preferred_element_type=jnp.float32
        )
        return partial_value.at[dst_index].add(products)

    partial_value = lax.fori_loop(0, tiles_here // batch_size, tile_batch, partial_zero)

    def grad_loop(step_pos, grad_state):
        return grad_move(grad_step(grad_state, step_pos))

    grad_state = lax.fori_loop(
        0, step_count - 1, grad_loop, jnp.zeros((src_blocks, tile_len, feat_width), jnp.float32)
    )
    grad_state = grad_step(grad_state, step_count - 1)
    summed = lax.psum_scatter(
        partial_value.reshape(dst_blocks * tile_len, feat_width).astype(jnp.bfloat16),
        "col",
        scatter_dimension=0,
        tiled=True,
    ).astype(jnp.float32)
    aggregated = (summed * dst_scale[:, None]).astype(jnp.bfloat16)
    grads = grad_state.reshape(src_blocks * tile_len, feat_width)
    feature_grad = (grads * src_scale[:, None]).astype(jnp.bfloat16)
    return (aggregated, feature_grad)


def solution(mesh):
    return jax.shard_map(
        local,
        mesh=mesh,
        in_specs=(
            P(("row", "col"), None),
            P(("row", "col"), None),
            P(("row", "col"), None, None),
            P(("row", "col"), None, None),
        ),
        out_specs=(P(("row", "col"), None), P(("row", "col"), None)),
        check_vma=False,
    )
```

profile of v0, /device:TPU:0, one launch (start us, length us, event | category | flops | bytes accessed | tf_op | source)
XLA Modules:
  0.0 244.0 jit_solution(11328118093270040016)
XLA Ops:
  7.2 0.8 fusion.26
  8.1 0.7 fusion.27
  8.8 0.7 fusion.29
  10.1 0.7 fusion.34
  10.8 0.7 copy.13
  11.5 1.3 dynamic-slice.2
  12.9 1.2 dynamic-slice
  15.8 2.3 convert_reduce_fusion
  18.3 8.4 %all-reduce = f32[512]{0:T(512)S(1)} all-reduce(f32[512]{0:T(512)S(1)} %convolution_bitcast_fusion.1), channel_id=3, replica_groups=mesh['row'=4,'col'=8] {'row'}, use_global_device_ids=true, to_apply=%region_5.6.clone | all-reduce | flops 512 | bytes 4096
  26.9 21.7 %all-reduce.1 = f32[1024]{0:T(1024)S(1)} all-reduce(f32[1024]{0:T(1024)S(1)} %convolution_bitcast_fusion), channel_id=5, replica_groups=mesh['row'=4,'col'=8] {'col'}, use_global_device_ids=true, to_apply=%region_11.12.clone | all-reduce | flops 1024 | bytes 8192
  48.8 31.5 %all_gather.7 = bf16[1024,256]{1,0:T(8,128)(2,1)S(1)} all-gather(bf16[128,256]{1,0:T(8,128)(2,1)S(1)} %multiply_convert_fusion), channel_id=1, replica_groups=mesh['row'=4,'col'=8] {'col'}, dimensions={0}, use_global_device_ids=true | all-gather | bytes 589824 | tf_op jit(solution)/shard_map/all_gather | solution.py:51
  80.3 1.7 gather_fusion.3
  82.1 2.0 gather_fusion.4
  84.1 5.0 %fusion.13 = f32[32,128,256]{2,1,0:T(8,128)} fusion(bf16[32,128,256]{2,1,0:T(8,128)(2,1)} %gather_fusion.4, bf16[32,128,128]{2,1,0:T(8,128)(2,1)} %gather_fusion.3, bf16[32]{0:T(256)(128)(2,1)S(1)} %fusion.26), kind=kOutput, calls=%fused_computation.41 | convolution fusion | flops 268959744 | bytes 7340096 | tf_op jit(solution)/shard_map/kij,kif->kjf/dot_general | solution.py:63
  89.0 49.5 %while.30 = (s32[]{:T(128)}, f32[1,128,256]{2,1,0:T(8,128)S(1)}, s32[4,3,32]{2,1,0:T(4,128)S(1)}, bf16[64,128,128]{2,1,0:T(8,128)(2,1)S(1)}, bf16[8,128,256]{2,1...) while((s32[]{:T(128)}, f32[1,128,256]{2,1,0:T(8,128)S(1)}, ...), condition=%wide.region_14.15_spmd.clone, body=%wide.region_12.14_spmd.clone.sunk | while | flops 270109056 | bytes 35530608 | solution.py:97
  89.1 1.7 gather_fusion.2
  91.6 4.3 %fusion.57 = f32[32,128,256]{2,1,0:T(8,128)} fusion(bf16[32,128,256]{2,1,0:T(8,128)(2,1)S(1)} %gather_fusion.1, bf16[32,128,128]{2,1,0:T(8,128)(2,1)} %gather_fusion.2, bf16[32]{0:T(256)(128)(2,1)S(1)} %fusion.56), kind=kOutput, calls=%fused_computation.17.clone.1 | convolution fusion | flops 268959744 | bytes 7340096 | tf_op jit(solution)/shard_map/while/body/eval_jaxpr/kij,kif->kjf/dot_general | solution.py:63
  95.9 6.4 %scatter_fusion.1 = f32[128,256,1]{1,0,2:T(8,128)S(1)} fusion(f32[128,256,1]{1,0,2:T(8,128)S(1)} %select_bitcast_fusion.2, s32[32]{0:T(128)S(1)} %fusion.54, f32[32,128,256]{2,1,0:T(8,128)} %fusion.57), kind=kCustom, calls=%fused_computation.6.clone.clone.1 | custom fusion | flops 1048576 | bytes 12583040 | tf_op jit(solution)/shard_map/while/body/eval_jaxpr/scatter-add | solution.py:66
  102.4 1.9 collective-permute-done
  104.5 1.7 gather_fusion.2
  106.9 4.3 %fusion.57 = f32[32,128,256]{2,1,0:T(8,128)} fusion(bf16[32,128,256]{2,1,0:T(8,128)(2,1)S(1)} %gather_fusion.1, bf16[32,128,128]{2,1,0:T(8,128)(2,1)} %gather_fusion.2, bf16[32]{0:T(256)(128)(2,1)S(1)} %fusion.56), kind=kOutput, calls=%fused_computation.17.clone.1 | convolution fusion | flops 268959744 | bytes 7340096 | tf_op jit(solution)/shard_map/while/body/eval_jaxpr/kij,kif->kjf/dot_general | solution.py:63
  111.2 6.4 %scatter_fusion.1 = f32[128,256,1]{1,0,2:T(8,128)S(1)} fusion(f32[128,256,1]{1,0,2:T(8,128)S(1)} %select_bitcast_fusion.2, s32[32]{0:T(128)S(1)} %fusion.54, f32[32,128,256]{2,1,0:T(8,128)} %fusion.57), kind=kCustom, calls=%fused_computation.6.clone.clone.1 | custom fusion | flops 1048576 | bytes 12583040 | tf_op jit(solution)/shard_map/while/body/eval_jaxpr/scatter-add | solution.py:66
  117.7 1.8 collective-permute-start
  119.5 1.9 collective-permute-done
  121.6 1.7 gather_fusion.2
  124.0 4.3 %fusion.57 = f32[32,128,256]{2,1,0:T(8,128)} fusion(bf16[32,128,256]{2,1,0:T(8,128)(2,1)S(1)} %gather_fusion.1, bf16[32,128,128]{2,1,0:T(8,128)(2,1)} %gather_fusion.2, bf16[32]{0:T(256)(128)(2,1)S(1)} %fusion.56), kind=kOutput, calls=%fused_computation.17.clone.1 | convolution fusion | flops 268959744 | bytes 7340096 | tf_op jit(solution)/shard_map/while/body/eval_jaxpr/kij,kif->kjf/dot_general | solution.py:63
  128.3 6.4 %scatter_fusion.1 = f32[128,256,1]{1,0,2:T(8,128)S(1)} fusion(f32[128,256,1]{1,0,2:T(8,128)S(1)} %select_bitcast_fusion.2, s32[32]{0:T(128)S(1)} %fusion.54, f32[32,128,256]{2,1,0:T(8,128)} %fusion.57), kind=kCustom, calls=%fused_computation.6.clone.clone.1 | custom fusion | flops 1048576 | bytes 12583040 | tf_op jit(solution)/shard_map/while/body/eval_jaxpr/scatter-add | solution.py:66
  134.8 1.8 collective-permute-start
  136.6 1.9 collective-permute-done
  138.6 6.3 %scatter_fusion.2 = f32[128,256,1]{1,0,2:T(8,128)S(1)} fusion(f32[128,256,1]{1,0,2:T(8,128)S(1)} %bitcast.83, s32[32]{0:T(128)S(1)} %fusion.27, f32[32,128,256]{2,1,0:T(8,128)} %fusion.13), kind=kCustom, calls=%fused_computation.7 | custom fusion | flops 1048576 | bytes 12583040 | tf_op jit(solution)/shard_map/scatter-add | solution.py:66
  144.9 0.7 fusion.16
  145.6 6.0 %all-gather = bf16[512,256]{1,0:T(8,128)(2,1)S(1)} all-gather(bf16[128,256]{1,0:T(8,128)(2,1)S(1)} %get-tuple-element.329), channel_id=2, replica_groups=mesh['row'=4,'col'=8] {'row'}, dimensions={0}, use_global_device_ids=true | all-gather | bytes 327680 | tf_op jit(solution)/shard_map/all_gather | solution.py:75
  151.7 23.5 %while.29 = (s32[]{:T(128)}, f32[8,128,256]{2,1,0:T(8,128)S(1)}, s32[64]{0:T(128)S(1)}, bf16[64,128,128]{2,1,0:T(8,128)(2,1)}, s32[64]{0:T(128)S(1)}, /*index=5*...) while((s32[]{:T(128)}, f32[8,128,256]{2,1,0:T(8,128)S(1)}, ...), condition=%wide.region_8.9_spmd, body=%wide.region_6.8_spmd.sunk | while | flops 135005296 | bytes 12063463 | solution.py:92
  151.9 1.6 gather_fusion
  153.5 1.9 fusion.51
  155.4 2.2 scatter_fusion
  157.7 1.6 gather_fusion
  159.3 1.9 fusion.51
  161.2 2.2 scatter_fusion
  163.6 1.6 gather_fusion
  165.2 1.9 fusion.51
  167.1 2.2 scatter_fusion
  169.5 1.6 gather_fusion
  171.1 1.9 fusion.51
  173.0 2.2 scatter_fusion
  175.2 0.8 convert_element_type.102
  176.0 59.6 %reduce-scatter.2.cloned.1.call-done = bf16[128,256]{1,0:T(8,128)(2,1)} async-done(((bf16[1024,256]{1,0:T(8,128)(2,1)}), bf16[128,256]{1,0:T(8,128)(2,1)}) %reduce-scatter.2.cloned.1.call-update) | async-done | bytes 65552 | tf_op jit(solution)/shard_map/reduce_scatter | solution.py:101
  235.6 1.6 multiply_convert_fusion.1
  (74 shorter events, 5.1 us)
Async XLA Ops:
  7.2 73.1 %copy-start = (bf16[64,128,128]{2,1,0:T(8,128)(2,1)S(1)}, bf16[64,128,128]{2,1,0:T(8,128)(2,1)}, u32[]{:S(2)}) copy-start(bf16[64,128,128]{2,1,0:T(8,128)(2,1)} %param.10) | copy-start | bytes 6291460
  7.2 41.5 %copy-start.3 = (bf16[128,256]{1,0:T(8,128)(2,1)S(1)}, bf16[128,256]{1,0:T(8,128)(2,1)}, u32[]{:S(2)}) copy-start(bf16[128,256]{1,0:T(8,128)(2,1)} %param.9) | copy-start | bytes 196612
  7.2 228.4 %reduce-scatter.2.cloned.1.call-start = ((), (), s32[]{:S(2)}) async-start(), calls=%async_computation.1 | async-start | bytes 589824 | tf_op jit(solution)/shard_map/reduce_scatter | solution.py:101
  95.9 8.4 %copy-start.1 = (bf16[64,128,128]{2,1,0:T(8,128)(2,1)S(1)}, bf16[64,128,128]{2,1,0:T(8,128)(2,1)}, u32[]{:S(2)}) copy-start(bf16[64,128,128]{2,1,0:T(8,128)(2,1)} %get-tuple-element.478) | copy-start | bytes 6291460 | tf_op jit(solution)/shard_map/while
  102.3 2.0 collective-permute-start
  111.2 10.2 %copy-start.1 = (bf16[64,128,128]{2,1,0:T(8,128)(2,1)S(1)}, bf16[64,128,128]{2,1,0:T(8,128)(2,1)}, u32[]{:S(2)}) copy-start(bf16[64,128,128]{2,1,0:T(8,128)(2,1)} %get-tuple-element.478) | copy-start | bytes 6291460 | tf_op jit(solution)/shard_map/while
  117.7 3.7 %collective-permute-start = (bf16[1,128,256]{2,1,0:T(8,128)(2,1)S(1)}, bf16[1,128,256]{2,1,0:T(8,128)(2,1)S(1)}, u32[]{:S(2)}, u32[]{:S(2)}) collective-permute-start(bf16[1,128,256]{2,1,0:T(8,128)(2,1)S(1)} %convert_bitcast_fusion.2), channel_id=1, source_target_pairs={{0,24},{8,0},{16,8},{24,16},{1,25},{9,1},{17,9},{25,17},{2,26},{10... | collective-permute-start | bytes 196616 | tf_op jit(solution)/shard_map/while/body/eval_jaxpr/ppermute | solution.py:11
  128.3 10.2 %copy-start.1 = (bf16[64,128,128]{2,1,0:T(8,128)(2,1)S(1)}, bf16[64,128,128]{2,1,0:T(8,128)(2,1)}, u32[]{:S(2)}) copy-start(bf16[64,128,128]{2,1,0:T(8,128)(2,1)} %get-tuple-element.478) | copy-start | bytes 6291460 | tf_op jit(solution)/shard_map/while
  134.8 3.7 %collective-permute-start = (bf16[1,128,256]{2,1,0:T(8,128)(2,1)S(1)}, bf16[1,128,256]{2,1,0:T(8,128)(2,1)S(1)}, u32[]{:S(2)}, u32[]{:S(2)}) collective-permute-start(bf16[1,128,256]{2,1,0:T(8,128)(2,1)S(1)} %convert_bitcast_fusion.2), channel_id=1, source_target_pairs={{0,24},{8,0},{16,8},{24,16},{1,25},{9,1},{17,9},{25,17},{2,26},{10... | collective-permute-start | bytes 196616 | tf_op jit(solution)/shard_map/while/body/eval_jaxpr/ppermute | solution.py:11
  138.6 6.4 %copy-start.2 = (bf16[128,256]{1,0:T(8,128)(2,1)S(1)}, bf16[128,256]{1,0:T(8,128)(2,1)}, u32[]{:S(2)}) copy-start(bf16[128,256]{1,0:T(8,128)(2,1)} %param.8) | copy-start | bytes 196612
Sparse Core Ops, SparseCore 0:
  176.1 59.4 reduce-scatter.1
where the time goes:
time: 245 us; the launch traced here: 244 us
  blocking collectives  67.5 us (28%)
  waiting for transfers between devices  65.3 us (27%)
  other arithmetic  43.9 us (18%)
  matrix products  25.9 us (11%)
  local copies, waits for them, and re-layouts  21.7 us (9%)
  between operations  15.4 us (6%)
  starting transfers between devices  3.77 us (2%)
    reduce_scatter x1, waiting for transfers between devices, local(): lax.psum_scatter(partial_value.reshape(dst_blocks * tile_len, feat_width)...  59.6 us
    all_gather x1, blocking collectives, local(): lax.all_gather(scaled_grads, 'col', axis=0, tiled=True)  31.5 us
    unnamed x2, blocking collectives  30 us
    scatter-add x4, other arithmetic, backward_add(): return accum_total.at[src_index].add(products)  25.6 us
    dot_general x4, matrix products, backward_add(): jnp.einsum('kij,kif->kjf', chosen, rows[dst_index], preferred_element_typ...  17.9 us
    scatter-add x4, other arithmetic, tile_batch(): return partial_value.at[dst_index].add(products)  8.78 us
    dot_general x4, matrix products, tile_batch(): jnp.einsum('kij,kjf->kif', chosen, everything[src_index], preferred_eleme...  7.47 us
    gather x4, local copies, waits for them, and re-layouts, pick_tiles(): chosen = tile_weight[jnp.maximum(tile_ids, 0)] * keep_mask[:, None, None]  6.93 us
  transfers between devices with their start and end apart: 4, of which 4 were waited for; matrix products, arithmetic and copies ran while one was open for 0% of the time, Pallas kernels for 0%

commit v1 on v0

--- a/solution.py
+++ b/solution.py
@@ -12,6 +12,31 @@
 
 
 def local(features, grad_out, tile_weight, tile_list):
+
+    def process_zone_in(message, along_axis):
+        val, b_next, front = (
+            jax.lax.axis_size(along_axis),
+            jax.lax.axis_index(along_axis),
+            message.shape[0],
+        )
+        made = [(src_i, (src_i + 1) % val) for src_i in range(val)]
+        placed = jnp.zeros((*message.shape[:0], val * front, *message.shape[1:]), message.dtype)
+        views = [(src_i, (src_i - 1) % val) for src_i in range(val)]
+        vec_out = v1 = message
+        placed = lax.dynamic_update_slice_in_dim(placed, message, b_next * front, axis=0)
+        part_next = val // 2
+        for q in range(1, part_next + 1):
+            vec_out = jax.lax.ppermute(vec_out, along_axis, made)
+            placed = lax.dynamic_update_slice_in_dim(
+                placed, vec_out, (b_next - q) % val * front, axis=0
+            )
+            if q < val - part_next:
+                v1 = jax.lax.ppermute(v1, along_axis, views)
+                placed = lax.dynamic_update_slice_in_dim(
+                    placed, v1, (b_next + q) % val * front, axis=0
+                )
+        return placed
+
     step_count = lax.axis_size("row")
     columns = lax.axis_size("col")
     row_pos = lax.axis_index("row")
@@ -48,9 +73,7 @@
     scaled = (features.astype(jnp.float32) * src_scale[:, None]).astype(jnp.bfloat16)
     scaled = scaled.reshape(src_blocks, tile_len, feat_width)
     scaled_grads = (grad_out.astype(jnp.float32) * dst_scale[:, None]).astype(jnp.bfloat16)
-    grad_rows = lax.all_gather(scaled_grads, "col", axis=0, tiled=True).reshape(
-        dst_blocks, tile_len, feat_width
-    )
+    grad_rows = process_zone_in(scaled_grads, "col").reshape(dst_blocks, tile_len, feat_width)
 
     def pick_tiles(list_step):
         tile_ids = tile_list[list_step, 0]

time: 245 us -> 234 us (0.955)
  blocking collectives: 67.5 us -> 35.1 us
  starting transfers between devices: 3.77 us -> 18 us
  waiting for transfers between devices: 65.3 us -> 77.3 us
  other arithmetic: 43.9 us -> 41.1 us
    all_gather x1 -> x0, blocking collectives: 31.5 us -> none  [local(): lax.all_gather(scaled_grads, 'col', axis=0, tiled=True)]
    ppermute x0 -> x7, starting transfers between devices: none -> 14.2 us  [the longest x3 14.2 us: process_zone_in(): v1 = jax.lax.ppermute(v1, along_axis, views)]
    ppermute x0 -> x7, waiting for transfers between devices: none -> 11.3 us  [the longest x4 11.3 us: process_zone_in(): vec_out = jax.lax.ppermute(vec_out, along_axis, made)]
  transfers between devices with their start and end apart: 4 -> 11, of which waited for: 4 -> 7; matrix products, arithmetic and copies ran while one was open for 0% -> 1% of each run, Pallas kernels for 0% -> 0%
where the time goes in v1:
time: 234 us
  waiting for transfers between devices  77.3 us (33%)
  other arithmetic  41.1 us (18%)
  blocking collectives  35.1 us (15%)
  matrix products  25.9 us (11%)
  local copies, waits for them, and re-layouts  20 us (9%)
  starting transfers between devices  18 us (8%)
  between operations  15.7 us (7%)
    reduce_scatter x1, waiting for transfers between devices, local(): lax.psum_scatter(partial_value.reshape(dst_blocks * tile_len, feat_width)...  60.3 us
    unnamed x2, blocking collectives  28.8 us
    scatter-add x4, other arithmetic, backward_add(): return accum_total.at[src_index].add(products)  25.6 us
    dot_general x4, matrix products, backward_add(): jnp.einsum('kij,kif->kjf', chosen, rows[dst_index], preferred_element_typ...  17.9 us
    ppermute x3, starting transfers between devices, process_zone_in(): v1 = jax.lax.ppermute(v1, along_axis, views)  14.2 us
    ppermute x4, waiting for transfers between devices, process_zone_in(): vec_out = jax.lax.ppermute(vec_out, along_axis, made)  11.3 us
    scatter-add x4, other arithmetic, tile_batch(): return partial_value.at[dst_index].add(products)  8.78 us
    dot_general x4, matrix products, tile_batch(): jnp.einsum('kij,kjf->kif', chosen, everything[src_index], preferred_eleme...  7.47 us
  transfers between devices with their start and end apart: 11, of which 7 were waited for; matrix products, arithmetic and copies ran while one was open for 1% of the time, Pallas kernels for 0%

profile of v1, /device:TPU:0, one launch (start us, length us, event | category | flops | bytes accessed | tf_op | source)
XLA Modules:
  0.0 233.6 jit_solution(13121410334265694236)
XLA Ops:
  7.3 0.9 fusion.34
  8.6 2.3 convert_reduce_fusion
  11.1 23.2 %all-reduce.1 = f32[1024]{0:T(1024)S(1)} all-reduce(f32[1024]{0:T(1024)S(1)} %convolution_bitcast_fusion), channel_id=5, replica_groups=mesh['row'=4,'col'=8] {'col'}, use_global_device_ids=true, to_apply=%region_11.12.clone | all-reduce | flops 1024 | bytes 8192
  35.8 4.7 %collective-permute-start.2 = (bf16[128,256]{1,0:T(8,128)(2,1)S(1)}, bf16[128,256]{1,0:T(8,128)(2,1)S(1)}, u32[]{:S(2)}, u32[]{:S(2)}) collective-permute-start(bf16[128,256]{1,0:T(8,128)(2,1)S(1)} %get-tuple-element.324), channel_id=1, source_target_pairs={{0,7},{1,0},{2,1},{3,2},{4,3},{5,4},{6,5},{7,6},{8,15},{9,8},{10,9... | collective-permute-start | bytes 196616 | tf_op jit(solution)/shard_map/ppermute | solution.py:34
  42.2 5.7 %all-reduce = f32[512]{0:T(512)S(1)} all-reduce(f32[512]{0:T(512)S(1)} %convolution_bitcast_fusion.1), channel_id=3, replica_groups=mesh['row'=4,'col'=8] {'row'}, use_global_device_ids=true, to_apply=%region_5.6.clone | all-reduce | flops 512 | bytes 4096
  47.9 1.7 gather_fusion.3
  49.7 4.7 %collective-permute-start.4 = (bf16[128,256]{1,0:T(8,128)(2,1)S(1)}, bf16[128,256]{1,0:T(8,128)(2,1)S(1)}, u32[]{:S(2)}, u32[]{:S(2)}) collective-permute-start(bf16[128,256]{1,0:T(8,128)(2,1)S(1)} %collective-permute-done.2), channel_id=1, source_target_pairs={{0,7},{1,0},{2,1},{3,2},{4,3},{5,4},{6,5},{7,6},{8,15},{9,8},{10,9... | collective-permute-start | bytes 196616 | tf_op jit(solution)/shard_map/ppermute | solution.py:34
  54.4 2.2 collective-permute-done.3
  56.6 4.7 %collective-permute-start.6 = (bf16[128,256]{1,0:T(8,128)(2,1)S(1)}, bf16[128,256]{1,0:T(8,128)(2,1)S(1)}, u32[]{:S(2)}, u32[]{:S(2)}) collective-permute-start(bf16[128,256]{1,0:T(8,128)(2,1)S(1)} %collective-permute-done.4), channel_id=1, source_target_pairs={{0,7},{1,0},{2,1},{3,2},{4,3},{5,4},{6,5},{7,6},{8,15},{9,8},{10,9... | collective-permute-start | bytes 196616 | tf_op jit(solution)/shard_map/ppermute | solution.py:34
  61.4 2.2 collective-permute-done.5
  63.6 6.9 %collective-permute-done.7 = bf16[128,256]{1,0:T(8,128)(2,1)S(1)} collective-permute-done((bf16[128,256]{1,0:T(8,128)(2,1)S(1)}, bf16[128,256]{1,0:T(8,128)(2,1)S(1)}, u32[]{:S(2)}, u32[]{:S(2)}) %collective-permute-start.7) | collective-permute-done | bytes 65568 | tf_op jit(solution)/shard_map/ppermute | solution.py:29
  70.6 2.0 gather_fusion.4
  72.6 5.0 %fusion.13 = f32[32,128,256]{2,1,0:T(8,128)} fusion(bf16[32,128,256]{2,1,0:T(8,128)(2,1)} %gather_fusion.4, bf16[32,128,128]{2,1,0:T(8,128)(2,1)} %gather_fusion.3, bf16[32]{0:T(256)(128)(2,1)S(1)} %fusion.26), kind=kOutput, calls=%fused_computation.41 | convolution fusion | flops 268959744 | bytes 7340096 | tf_op jit(solution)/shard_map/kij,kif->kjf/dot_general | solution.py:86
  77.6 49.5 %while.30 = (s32[]{:T(128)}, f32[1,128,256]{2,1,0:T(8,128)S(1)}, s32[4,3,32]{2,1,0:T(4,128)S(1)}, bf16[64,128,128]{2,1,0:T(8,128)(2,1)S(1)}, bf16[8,128,256]{2,1...) while((s32[]{:T(128)}, f32[1,128,256]{2,1,0:T(8,128)S(1)}, ...), condition=%wide.region_14.15_spmd.clone, body=%wide.region_12.14_spmd.clone.sunk | while | flops 270109056 | bytes 35530608 | solution.py:120
  77.7 1.7 gather_fusion.2
  79.4 0.7 gather_fusion.1
  80.1 4.3 %fusion.57 = f32[32,128,256]{2,1,0:T(8,128)} fusion(bf16[32,128,256]{2,1,0:T(8,128)(2,1)S(1)} %gather_fusion.1, bf16[32,128,128]{2,1,0:T(8,128)(2,1)} %gather_fusion.2, bf16[32]{0:T(256)(128)(2,1)S(1)} %fusion.56), kind=kOutput, calls=%fused_computation.17.clone.1 | convolution fusion | flops 268959744 | bytes 7340096 | tf_op jit(solution)/shard_map/while/body/eval_jaxpr/kij,kif->kjf/dot_general | solution.py:86
  84.4 6.4 %scatter_fusion.1 = f32[128,256,1]{1,0,2:T(8,128)S(1)} fusion(f32[128,256,1]{1,0,2:T(8,128)S(1)} %select_bitcast_fusion.2, s32[32]{0:T(128)S(1)} %fusion.54, f32[32,128,256]{2,1,0:T(8,128)} %fusion.57), kind=kCustom, calls=%fused_computation.6.clone.clone.1 | custom fusion | flops 1048576 | bytes 12583040 | tf_op jit(solution)/shard_map/while/body/eval_jaxpr/scatter-add | solution.py:89
  90.9 1.9 collective-permute-done
  93.0 1.7 gather_fusion.2
  95.4 4.3 %fusion.57 = f32[32,128,256]{2,1,0:T(8,128)} fusion(bf16[32,128,256]{2,1,0:T(8,128)(2,1)S(1)} %gather_fusion.1, bf16[32,128,128]{2,1,0:T(8,128)(2,1)} %gather_fusion.2, bf16[32]{0:T(256)(128)(2,1)S(1)} %fusion.56), kind=kOutput, calls=%fused_computation.17.clone.1 | convolution fusion | flops 268959744 | bytes 7340096 | tf_op jit(solution)/shard_map/while/body/eval_jaxpr/kij,kif->kjf/dot_general | solution.py:86
  99.7 6.4 %scatter_fusion.1 = f32[128,256,1]{1,0,2:T(8,128)S(1)} fusion(f32[128,256,1]{1,0,2:T(8,128)S(1)} %select_bitcast_fusion.2, s32[32]{0:T(128)S(1)} %fusion.54, f32[32,128,256]{2,1,0:T(8,128)} %fusion.57), kind=kCustom, calls=%fused_computation.6.clone.clone.1 | custom fusion | flops 1048576 | bytes 12583040 | tf_op jit(solution)/shard_map/while/body/eval_jaxpr/scatter-add | solution.py:89
  106.2 1.8 collective-permute-start
  108.0 1.9 collective-permute-done
  110.1 1.7 gather_fusion.2
  112.5 4.3 %fusion.57 = f32[32,128,256]{2,1,0:T(8,128)} fusion(bf16[32,128,256]{2,1,0:T(8,128)(2,1)S(1)} %gather_fusion.1, bf16[32,128,128]{2,1,0:T(8,128)(2,1)} %gather_fusion.2, bf16[32]{0:T(256)(128)(2,1)S(1)} %fusion.56), kind=kOutput, calls=%fused_computation.17.clone.1 | convolution fusion | flops 268959744 | bytes 7340096 | tf_op jit(solution)/shard_map/while/body/eval_jaxpr/kij,kif->kjf/dot_general | solution.py:86
  116.8 6.4 %scatter_fusion.1 = f32[128,256,1]{1,0,2:T(8,128)S(1)} fusion(f32[128,256,1]{1,0,2:T(8,128)S(1)} %select_bitcast_fusion.2, s32[32]{0:T(128)S(1)} %fusion.54, f32[32,128,256]{2,1,0:T(8,128)} %fusion.57), kind=kCustom, calls=%fused_computation.6.clone.clone.1 | custom fusion | flops 1048576 | bytes 12583040 | tf_op jit(solution)/shard_map/while/body/eval_jaxpr/scatter-add | solution.py:89
  123.3 1.8 collective-permute-start
  125.1 1.9 collective-permute-done
  127.1 6.3 %scatter_fusion.2 = f32[128,256,1]{1,0,2:T(8,128)S(1)} fusion(f32[128,256,1]{1,0,2:T(8,128)S(1)} %bitcast.83, s32[32]{0:T(128)S(1)} %fusion.27, f32[32,128,256]{2,1,0:T(8,128)} %fusion.13), kind=kCustom, calls=%fused_computation.7 | custom fusion | flops 1048576 | bytes 12583040 | tf_op jit(solution)/shard_map/scatter-add | solution.py:89
  133.4 0.7 fusion.16
  134.1 6.3 %all-gather = bf16[512,256]{1,0:T(8,128)(2,1)S(1)} all-gather(bf16[128,256]{1,0:T(8,128)(2,1)S(1)} %get-tuple-element.331), channel_id=2, replica_groups=mesh['row'=4,'col'=8] {'row'}, dimensions={0}, use_global_device_ids=true | all-gather | bytes 327680 | tf_op jit(solution)/shard_map/all_gather | solution.py:98
  140.6 23.5 %while.29 = (s32[]{:T(128)}, f32[8,128,256]{2,1,0:T(8,128)S(1)}, s32[64]{0:T(128)S(1)}, bf16[64,128,128]{2,1,0:T(8,128)(2,1)}, s32[64]{0:T(128)S(1)}, /*index=5*...) while((s32[]{:T(128)}, f32[8,128,256]{2,1,0:T(8,128)S(1)}, ...), condition=%wide.region_8.9_spmd, body=%wide.region_6.8_spmd.sunk | while | flops 135005296 | bytes 12063463 | solution.py:115
  140.7 1.6 gather_fusion
  142.3 1.9 fusion.51
  144.2 2.2 scatter_fusion
  146.6 1.6 gather_fusion
  148.2 1.9 fusion.51
  150.1 2.2 scatter_fusion
  152.5 1.6 gather_fusion
  154.1 1.9 fusion.51
  156.0 2.2 scatter_fusion
  158.4 1.6 gather_fusion
  160.0 1.9 fusion.51
  161.8 2.2 scatter_fusion
  164.0 0.8 convert_element_type.102
  164.9 60.3 %reduce-scatter.2.cloned.1.call-done = bf16[128,256]{1,0:T(8,128)(2,1)} async-done(((bf16[1024,256]{1,0:T(8,128)(2,1)}), bf16[128,256]{1,0:T(8,128)(2,1)}) %reduce-scatter.2.cloned.1.call-update) | async-done | bytes 65552 | tf_op jit(solution)/shard_map/reduce_scatter | solution.py:124
  225.2 1.6 multiply_convert_fusion.1
  (101 shorter events, 5.2 us)
Async XLA Ops:
  7.2 27.1 %copy-start.6 = (u32[32]{0:T(128)S(1)}, u32[32]{0:T(128)}, u32[]{:S(2)}) copy-start(u32[32]{0:T(128)} %constant.228) | copy-start | bytes 388
  7.2 33.4 %copy-start.5 = (u32[32]{0:T(128)S(1)}, u32[32]{0:T(128)}, u32[]{:S(2)}) copy-start(u32[32]{0:T(128)} %constant.224) | copy-start | bytes 388
  7.2 33.3 %copy-start.4 = (s32[4,3,32]{2,0,1:T(4,128)S(1)}, s32[4,3,32]{2,0,1:T(4,128)}, u32[]{:S(2)}) copy-start(s32[4,3,32]{2,0,1:T(4,128)} %param.11) | copy-start | bytes 4612
  7.2 40.7 %copy-start = (bf16[64,128,128]{2,1,0:T(8,128)(2,1)S(1)}, bf16[64,128,128]{2,1,0:T(8,128)(2,1)}, u32[]{:S(2)}) copy-start(bf16[64,128,128]{2,1,0:T(8,128)(2,1)} %param.10) | copy-start | bytes 6291460
  7.2 28.4 %copy-start.2 = (bf16[128,256]{1,0:T(8,128)(2,1)S(1)}, bf16[128,256]{1,0:T(8,128)(2,1)}, u32[]{:S(2)}) copy-start(bf16[128,256]{1,0:T(8,128)(2,1)} %param.9) | copy-start | bytes 196612
  7.2 218.0 %reduce-scatter.2.cloned.1.call-start = ((), (), s32[]{:S(2)}) async-start(), calls=%async_computation.1 | async-start | bytes 589824 | tf_op jit(solution)/shard_map/reduce_scatter | solution.py:124
  35.7 13.9 %collective-permute-start.1 = (bf16[128,256]{1,0:T(8,128)(2,1)S(1)}, bf16[128,256]{1,0:T(8,128)(2,1)S(1)}, u32[]{:S(2)}, u32[]{:S(2)}) collective-permute-start(bf16[128,256]{1,0:T(8,128)(2,1)S(1)} %get-tuple-element.324), channel_id=1, source_target_pairs={{0,1},{1,2},{2,3},{3,4},{4,5},{5,6},{6,7},{7,0},{8,9},{9,10},{10,1... | collective-permute-start | bytes 196616 | tf_op jit(solution)/shard_map/ppermute | solution.py:29
  35.8 13.9 %collective-permute-start.2 = (bf16[128,256]{1,0:T(8,128)(2,1)S(1)}, bf16[128,256]{1,0:T(8,128)(2,1)S(1)}, u32[]{:S(2)}, u32[]{:S(2)}) collective-permute-start(bf16[128,256]{1,0:T(8,128)(2,1)S(1)} %get-tuple-element.324), channel_id=1, source_target_pairs={{0,7},{1,0},{2,1},{3,2},{4,3},{5,4},{6,5},{7,6},{8,15},{9,8},{10,9... | collective-permute-start | bytes 196616 | tf_op jit(solution)/shard_map/ppermute | solution.py:34
  49.7 7.0 %collective-permute-start.3 = (bf16[128,256]{1,0:T(8,128)(2,1)S(1)}, bf16[128,256]{1,0:T(8,128)(2,1)S(1)}, u32[]{:S(2)}, u32[]{:S(2)}) collective-permute-start(bf16[128,256]{1,0:T(8,128)(2,1)S(1)} %collective-permute-done.1), channel_id=1, source_target_pairs={{0,1},{1,2},{2,3},{3,4},{4,5},{5,6},{6,7},{7,0},{8,9},{9,10},{10,1... | collective-permute-start | bytes 196616 | tf_op jit(solution)/shard_map/ppermute | solution.py:29
  49.7 7.0 %collective-permute-start.4 = (bf16[128,256]{1,0:T(8,128)(2,1)S(1)}, bf16[128,256]{1,0:T(8,128)(2,1)S(1)}, u32[]{:S(2)}, u32[]{:S(2)}) collective-permute-start(bf16[128,256]{1,0:T(8,128)(2,1)S(1)} %collective-permute-done.2), channel_id=1, source_target_pairs={{0,7},{1,0},{2,1},{3,2},{4,3},{5,4},{6,5},{7,6},{8,15},{9,8},{10,9... | collective-permute-start | bytes 196616 | tf_op jit(solution)/shard_map/ppermute | solution.py:34
  56.6 7.0 %collective-permute-start.5 = (bf16[128,256]{1,0:T(8,128)(2,1)S(1)}, bf16[128,256]{1,0:T(8,128)(2,1)S(1)}, u32[]{:S(2)}, u32[]{:S(2)}) collective-permute-start(bf16[128,256]{1,0:T(8,128)(2,1)S(1)} %collective-permute-done.3), channel_id=1, source_target_pairs={{0,1},{1,2},{2,3},{3,4},{4,5},{5,6},{6,7},{7,0},{8,9},{9,10},{10,1... | collective-permute-start | bytes 196616 | tf_op jit(solution)/shard_map/ppermute | solution.py:29
  56.6 7.0 %collective-permute-start.6 = (bf16[128,256]{1,0:T(8,128)(2,1)S(1)}, bf16[128,256]{1,0:T(8,128)(2,1)S(1)}, u32[]{:S(2)}, u32[]{:S(2)}) collective-permute-start(bf16[128,256]{1,0:T(8,128)(2,1)S(1)} %collective-permute-done.4), channel_id=1, source_target_pairs={{0,7},{1,0},{2,1},{3,2},{4,3},{5,4},{6,5},{7,6},{8,15},{9,8},{10,9... | collective-permute-start | bytes 196616 | tf_op jit(solution)/shard_map/ppermute | solution.py:34
  63.6 7.0 %collective-permute-start.7 = (bf16[128,256]{1,0:T(8,128)(2,1)S(1)}, bf16[128,256]{1,0:T(8,128)(2,1)S(1)}, u32[]{:S(2)}, u32[]{:S(2)}) collective-permute-start(bf16[128,256]{1,0:T(8,128)(2,1)S(1)} %collective-permute-done.5), channel_id=1, source_target_pairs={{0,1},{1,2},{2,3},{3,4},{4,5},{5,6},{6,7},{7,0},{8,9},{9,10},{10,1... | collective-permute-start | bytes 196616 | tf_op jit(solution)/shard_map/ppermute | solution.py:29
  84.4 8.4 %copy-start.1 = (bf16[64,128,128]{2,1,0:T(8,128)(2,1)S(1)}, bf16[64,128,128]{2,1,0:T(8,128)(2,1)}, u32[]{:S(2)}) copy-start(bf16[64,128,128]{2,1,0:T(8,128)(2,1)} %get-tuple-element.480) | copy-start | bytes 6291460 | tf_op jit(solution)/shard_map/while
  90.8 2.0 collective-permute-start
  99.7 10.2 %copy-start.1 = (bf16[64,128,128]{2,1,0:T(8,128)(2,1)S(1)}, bf16[64,128,128]{2,1,0:T(8,128)(2,1)}, u32[]{:S(2)}) copy-start(bf16[64,128,128]{2,1,0:T(8,128)(2,1)} %get-tuple-element.480) | copy-start | bytes 6291460 | tf_op jit(solution)/shard_map/while
  106.2 3.7 %collective-permute-start = (bf16[1,128,256]{2,1,0:T(8,128)(2,1)S(1)}, bf16[1,128,256]{2,1,0:T(8,128)(2,1)S(1)}, u32[]{:S(2)}, u32[]{:S(2)}) collective-permute-start(bf16[1,128,256]{2,1,0:T(8,128)(2,1)S(1)} %convert_bitcast_fusion.2), channel_id=1, source_target_pairs={{0,24},{8,0},{16,8},{24,16},{1,25},{9,1},{17,9},{25,17},{2,26},{10... | collective-permute-start | bytes 196616 | tf_op jit(solution)/shard_map/while/body/eval_jaxpr/ppermute | solution.py:11
  116.8 10.2 %copy-start.1 = (bf16[64,128,128]{2,1,0:T(8,128)(2,1)S(1)}, bf16[64,128,128]{2,1,0:T(8,128)(2,1)}, u32[]{:S(2)}) copy-start(bf16[64,128,128]{2,1,0:T(8,128)(2,1)} %get-tuple-element.480) | copy-start | bytes 6291460 | tf_op jit(solution)/shard_map/while
  123.3 3.7 %collective-permute-start = (bf16[1,128,256]{2,1,0:T(8,128)(2,1)S(1)}, bf16[1,128,256]{2,1,0:T(8,128)(2,1)S(1)}, u32[]{:S(2)}, u32[]{:S(2)}) collective-permute-start(bf16[1,128,256]{2,1,0:T(8,128)(2,1)S(1)} %convert_bitcast_fusion.2), channel_id=1, source_target_pairs={{0,24},{8,0},{16,8},{24,16},{1,25},{9,1},{17,9},{25,17},{2,26},{10... | collective-permute-start | bytes 196616 | tf_op jit(solution)/shard_map/while/body/eval_jaxpr/ppermute | solution.py:11
  127.1 6.4 %copy-start.3 = (bf16[128,256]{1,0:T(8,128)(2,1)S(1)}, bf16[128,256]{1,0:T(8,128)(2,1)}, u32[]{:S(2)}) copy-start(bf16[128,256]{1,0:T(8,128)(2,1)} %param.8) | copy-start | bytes 196612
Sparse Core Ops, SparseCore 0:
  165.0 60.1 reduce-scatter.1
